TPU v7x, 256 devices: a whole 4x4x8 slice. The times are simulated.
256 devices in a mesh: pairs: 16 (over z, core), cols: 16 (over y, x).
Axes of the slice: x: 4, y: 4, z: 8, core: 2. Of those that a mesh axis runs over, the one named last changes fastest.
Arguments:
- pair_list: int32 [96, 5], P('pairs'), may hold values from 0 to 15, as said below
- near_tile_block: bfloat16 [96, 2048, 2048], P('pairs', None, 'cols'), may hold values from -0.0546875 to 0.0546875
- history: float32 [4, 32, 32, 2048], P(None, 'pairs', None, 'cols'), may hold values from -6 to 6
- excitation: float32 [4, 32, 32, 2048], P(None, 'pairs', None, 'cols'), may hold values from -6 to 6
- diagonal: float32 [32, 2048], P('pairs', 'cols'), may hold values from 2 to 4
Outputs:
- densities: float32 [4, 32, 32, 2048], P(None, 'pairs', None, 'cols')
Inputs may be any that keep to these rules, and one draw needn't show every extreme that they name: `pair_list`: rows s * 6 to s * 6 + 5 are the slots of index s of pairs. Column 0 and column 2 are below 2, column 1 below 16, column 3 below 4, column 4 is 0 or 1. The live slots of a device come first and number at least 3; among them no value of column 1 appears more than 3 times, and some value exactly 3 times. One device has all 6 slots live.
All inputs are finite; a program needn't handle non-finite values.
Results may differ from a plain program's by a relative error of at most 0.0018.
Values may be sent and summed in bfloat16 or wider, within the bound.
A program may use at most 64 MiB of HBM per device.

v0:
```python
import jax
import jax.numpy as jnp
from jax import lax
from jax.sharding import PartitionSpec as P

SM = 3
STEPS = 4


def shards(pair_list, near_tile_block, history, excitation, diagonal):
    groups = lax.axis_size("pairs")
    delays, clusters, excite, width = history.shape
    buffer_rows = groups * SM
    first_local = pair_list[:, 0]
    owners = pair_list[:, 1]
    second_local = pair_list[:, 2]
    delay_index = pair_list[:, 3]
    live = pair_list[:, 4] == 1
    live_float = live.astype(jnp.float32)
    owner_hits = ((owners[:, None] == jnp.arange(groups)[None, :]) & live[:, None]).astype(
        jnp.int32
    )
    rank = jnp.sum(jnp.cumsum(owner_hits, axis=0) * owner_hits, axis=1) - 1
    position = jnp.where(live, owners * SM + rank, buffer_rows)
    codes = jnp.full((buffer_rows,), -1, jnp.int32)
    codes = codes.at[position].set(delay_index * clusters + second_local, mode="drop")
    wanted = lax.all_to_all(
        codes.reshape(groups, SM), "pairs", split_axis=0, concat_axis=0, tiled=True
    ).reshape(buffer_rows)
    wanted_valid = wanted >= 0
    wanted_index = jnp.maximum(wanted, 0)
    back_table = (
        (wanted_index[None, :] % clusters == jnp.arange(clusters)[:, None]) & wanted_valid[None, :]
    ).astype(jnp.float32)
    first_table = (first_local[None, :] == jnp.arange(clusters)[:, None]).astype(
        jnp.float32
    ) * live_float[None, :]
    slot_source = jnp.minimum(position, buffer_rows - 1)
    own_index = delay_index * clusters + first_local
    results = []
    for step in range(STEPS):
        rounded = history.astype(jnp.bfloat16)
        flat = rounded.reshape(delays * clusters, excite, width)
        outgoing = jnp.where(
            wanted_valid[:, None, None],
            jnp.take(flat, wanted_index, axis=0),
            jnp.zeros((), jnp.bfloat16),
        )
        incoming = lax.all_to_all(
            outgoing.reshape(groups, SM, excite, width),
            "pairs",
            split_axis=0,
            concat_axis=0,
            tiled=True,
        )
        remote = jnp.take(incoming.reshape(buffer_rows, excite, width), slot_source, axis=0)
        forward = jnp.einsum(
            "sek,smk->sem", remote, near_tile_block, preferred_element_type=jnp.float32
        )
        forward_sum = jnp.einsum(
            "cs,sem->cem", first_table, forward, precision=lax.Precision.HIGHEST
        )
        collected = lax.all_gather(rounded, "cols", axis=3, tiled=True)
        near_rows = jnp.take(collected.reshape(delays * clusters, excite, -1), own_index, axis=0)
        backward = jnp.einsum(
            "sem,smk->sek", near_rows, near_tile_block, preferred_element_type=jnp.float32
        )
        backward = backward * live_float[:, None, None]
        outbound = (
            jnp.zeros((buffer_rows, excite, width), jnp.float32)
            .at[position]
            .set(backward, mode="drop")
        )
        received = lax.all_to_all(
            outbound.reshape(groups, SM, excite, width),
            "pairs",
            split_axis=0,
            concat_axis=0,
            tiled=True,
        )
        backward_sum = jnp.einsum(
            "cq,qek->cek",
            back_table,
            received.reshape(buffer_rows, excite, width),
            precision=lax.Precision.HIGHEST,
        )
        total = lax.psum(forward_sum, "cols")
        own_part = lax.dynamic_slice_in_dim(total, lax.axis_index("cols") * width, width, 2)
        field = own_part + backward_sum
        fresh = (excitation[step] - field) / diagonal[:, None, :]
        results.append(fresh)
        history = jnp.concatenate([fresh[None], history[:-1]], axis=0)
    return jnp.stack(results)


def solution(mesh):
    placed = (
        P("pairs", None),
        P("pairs", None, "cols"),
        P(None, "pairs", None, "cols"),
        P(None, "pairs", None, "cols"),
        P("pairs", "cols"),
    )
    return jax.shard_map(
        shards,
        mesh=mesh,
        in_specs=placed,
        out_specs=P(None, "pairs", None, "cols"),
        check_vma=False,
    )
```

profile of v0, /device:TPU:2, one launch (start us, length us, event | category | flops | bytes accessed | tf_op | source)
XLA Modules:
  0.0 696.8 jit_solution(621412180078924286)
XLA Ops:
  6.5 1.7 convert_element_type.42
  8.3 1.1 slice_reduce_fusion
  11.3 16.0 %all_to_all.49 = s32[16,1,3]{2,1,0:T(1,128)S(1)} all-to-all(s32[16,1,3]{2,1,0:T(1,128)S(1)} %bitcast.106), channel_id=1, replica_groups=mesh['pairs'=16,'cols'=16] {'pairs'}, dimensions={0} | all-to-all | bytes 384 | tf_op jit(solution)/shard_map/all_to_all | solution.py:27
  28.7 1.6 gather_fusion
  30.9 0.9 select_select_fusion.3
  31.9 3.6 all-to-all-start.1
  35.4 1.2 compare_and_fusion
  37.2 23.3 %all-gather.5.cloned.1.call-done = bf16[4,2,32,2048]{3,2,1,0:T(8,128)(2,1)} async-done(((bf16[4,2,32,128]{3,2,1,0:T(8,128)(2,1)}), bf16[4,2,32,2048]{3,2,1,0:T(8,128)(2,1)}) %all-gather.5.cloned.1.call-update) | async-done | bytes 1048592 | tf_op jit(solution)/shard_map/all_gather | solution.py:63
  60.5 2.8 gather_fusion.2
  63.4 2.4 convolution_multiply_fusion.3
  65.8 1.0 broadcast.143.clone
  66.8 2.2 scatter_fusion
  69.0 7.2 %all-to-all-start.2 = ((f32[16,3,32,128]{3,2,1,0:T(8,128)}), f32[16,3,32,128]{3,2,1,0:T(8,128)}, u32[]{:S(2)}, u32[]{:S(2)}) async-start(f32[16,3,32,128]{3,2,1,0:T(8,128)} %bitcast.95), calls=%async_computation.2 | async-start | bytes 1572864 | tf_op jit(solution)/shard_map/all_to_all | solution.py:74
  76.3 0.7 compare_and_fusion.1
  77.6 1.3 gather_fusion.1
  78.9 2.0 fusion.46
  80.9 3.5 fusion.6
  84.5 0.9 slice.43
  85.4 0.6 fusion.79
  86.1 93.7 %all-reduce.5.cloned.1.call-done = f32[2,32,2048]{2,0,1:T(2,128)} async-done(((f32[2,32,2048]{2,0,1:T(2,128)}), f32[2,32,2048]{2,0,1:T(2,128)}) %all-reduce.5.cloned.1.call-update) | async-done | bytes 524304 | tf_op jit(solution)/shard_map/psum | solution.py:87
  179.8 1.9 fusion.19
  183.0 1.6 gather_fusion.3
  184.6 1.6 select_select_fusion.2
  186.2 7.1 %all-to-all-start.3 = ((bf16[16,3,32,128]{3,2,1,0:T(8,128)(2,1)}), bf16[16,3,32,128]{3,2,1,0:T(8,128)(2,1)S(1)}, u32[]{:S(2)}, u32[]{:S(2)}) async-start(bf16[16,3,32,128]{3,2,1,0:T(8,128)(2,1)} %bitcast.17), calls=%async_computation.3 | async-start | bytes 786432 | tf_op jit(solution)/shard_map/all_to_all | solution.py:49
  193.3 37.5 %all-gather.7.cloned.1.call-done = bf16[4,2,32,2048]{3,2,1,0:T(8,128)(2,1)} async-done(((bf16[4,2,32,128]{3,2,1,0:T(8,128)(2,1)}), bf16[4,2,32,2048]{3,2,1,0:T(8,128)(2,1)}) %all-gather.7.cloned.1.call-update) | async-done | bytes 1048592 | tf_op jit(solution)/shard_map/all_gather | solution.py:63
  230.7 2.8 gather_fusion.5
  233.6 2.4 convolution_multiply_fusion.2
  236.0 1.0 broadcast.143.clone.1
  237.0 2.3 scatter_fusion.1
  239.4 7.2 %all-to-all-start.4 = ((f32[16,3,32,128]{3,2,1,0:T(8,128)}), f32[16,3,32,128]{3,2,1,0:T(8,128)}, u32[]{:S(2)}, u32[]{:S(2)}) async-start(f32[16,3,32,128]{3,2,1,0:T(8,128)} %bitcast.96), calls=%async_computation.4 | async-start | bytes 1572864 | tf_op jit(solution)/shard_map/all_to_all | solution.py:74
  246.8 1.3 gather_fusion.4
  248.1 2.0 fusion.44
  250.1 3.5 fusion.4
  253.7 95.3 %all-reduce.7.cloned.1.call-done = f32[2,32,2048]{2,0,1:T(2,128)} async-done(((f32[2,32,2048]{2,0,1:T(2,128)}), f32[2,32,2048]{2,0,1:T(2,128)}) %all-reduce.7.cloned.1.call-update) | async-done | bytes 524304 | tf_op jit(solution)/shard_map/psum | solution.py:87
  349.0 1.9 fusion.16
  352.2 1.6 gather_fusion.6
  353.8 1.6 select_select_fusion.1
  355.4 7.1 %all-to-all-start.5 = ((bf16[16,3,32,128]{3,2,1,0:T(8,128)(2,1)}), bf16[16,3,32,128]{3,2,1,0:T(8,128)(2,1)S(1)}, u32[]{:S(2)}, u32[]{:S(2)}) async-start(bf16[16,3,32,128]{3,2,1,0:T(8,128)(2,1)} %bitcast.25), calls=%async_computation.5 | async-start | bytes 786432 | tf_op jit(solution)/shard_map/all_to_all | solution.py:49
  362.5 37.5 %all-gather.9.cloned.1.call-done = bf16[4,2,32,2048]{3,2,1,0:T(8,128)(2,1)} async-done(((bf16[4,2,32,128]{3,2,1,0:T(8,128)(2,1)}), bf16[4,2,32,2048]{3,2,1,0:T(8,128)(2,1)}) %all-gather.9.cloned.1.call-update) | async-done | bytes 1048592 | tf_op jit(solution)/shard_map/all_gather | solution.py:63
  400.0 2.8 gather_fusion.8
  402.8 2.4 convolution_multiply_fusion.1
  405.3 1.0 broadcast.143.clone.2
  406.3 2.3 scatter_fusion.2
  408.6 7.2 %all-to-all-start.6 = ((f32[16,3,32,128]{3,2,1,0:T(8,128)}), f32[16,3,32,128]{3,2,1,0:T(8,128)}, u32[]{:S(2)}, u32[]{:S(2)}) async-start(f32[16,3,32,128]{3,2,1,0:T(8,128)} %bitcast.97), calls=%async_computation.6 | async-start | bytes 1572864 | tf_op jit(solution)/shard_map/all_to_all | solution.py:74
  415.8 1.3 gather_fusion.7
  417.2 2.0 fusion.42
  419.2 3.5 fusion.2
  422.8 95.3 %all-reduce.9.cloned.1.call-done = f32[2,32,2048]{2,0,1:T(2,128)} async-done(((f32[2,32,2048]{2,0,1:T(2,128)}), f32[2,32,2048]{2,0,1:T(2,128)}) %all-reduce.9.cloned.1.call-update) | async-done | bytes 524304 | tf_op jit(solution)/shard_map/psum | solution.py:87
  518.1 1.9 fusion.13
  521.3 1.6 gather_fusion.9
  522.9 1.6 select_select_fusion
  524.5 7.1 %all-to-all-start.7 = ((bf16[16,3,32,128]{3,2,1,0:T(8,128)(2,1)}), bf16[16,3,32,128]{3,2,1,0:T(8,128)(2,1)S(1)}, u32[]{:S(2)}, u32[]{:S(2)}) async-start(bf16[16,3,32,128]{3,2,1,0:T(8,128)(2,1)} %bitcast.33), calls=%async_computation.7 | async-start | bytes 786432 | tf_op jit(solution)/shard_map/all_to_all | solution.py:49
  531.6 37.5 %all-gather.11.cloned.1.call-done = bf16[4,2,32,2048]{3,2,1,0:T(8,128)(2,1)} async-done(((bf16[4,2,32,128]{3,2,1,0:T(8,128)(2,1)}), bf16[4,2,32,2048]{3,2,1,0:T(8,128)(2,1)}) %all-gather.11.cloned.1.call-update) | async-done | bytes 1048592 | tf_op jit(solution)/shard_map/all_gather | solution.py:63
  569.1 2.8 gather_fusion.11
  571.9 2.4 convolution_multiply_fusion
  574.4 1.0 broadcast.143
  575.3 2.2 scatter_fusion.3
  577.6 7.2 %all-to-all-start.8 = ((f32[16,3,32,128]{3,2,1,0:T(8,128)}), f32[16,3,32,128]{3,2,1,0:T(8,128)}, u32[]{:S(2)}, u32[]{:S(2)}) async-start(f32[16,3,32,128]{3,2,1,0:T(8,128)} %bitcast.94), calls=%async_computation.8 | async-start | bytes 1572864 | tf_op jit(solution)/shard_map/all_to_all | solution.py:74
  585.0 1.3 gather_fusion.10
  586.3 2.0 fusion.40
  588.4 3.5 fusion
  591.9 95.3 %all-reduce.11.cloned.1.call-done = f32[2,32,2048]{2,0,1:T(2,128)} async-done(((f32[2,32,2048]{2,0,1:T(2,128)}), f32[2,32,2048]{2,0,1:T(2,128)}) %all-reduce.11.cloned.1.call-update) | async-done | bytes 524304 | tf_op jit(solution)/shard_map/psum | solution.py:87
  687.3 1.9 fusion.10
  689.3 0.7 copy.67
  (139 shorter events, 10.0 us)
Async XLA Ops:
  6.5 56.9 %copy-start = (bf16[6,2048,128]{2,1,0:T(8,128)(2,1)S(1)}, bf16[6,2048,128]{2,1,0:T(8,128)(2,1)}, u32[]{:S(2)}) copy-start(bf16[6,2048,128]{2,1,0:T(8,128)(2,1)} %param.12) | copy-start | bytes 9437188
  6.5 54.0 %all-gather.5.cloned.1.call-start = ((), (), s32[]{:S(2)}) async-start(), calls=%async_computation.10 | async-start | bytes 1114112 | tf_op jit(solution)/shard_map/all_gather | solution.py:63
  9.3 0.5 copy-start.40
  9.4 71.5 %copy-start.19 = (s32[6]{0:T(128)}, s32[6]{0:T(128)S(1)}, u32[]{:S(2)}) copy-start(s32[6]{0:T(128)S(1)} %get-tuple-element.8) | copy-start | bytes 76
  9.5 0.6 copy-start.38
  9.5 71.4 %copy-start.15 = (f32[6]{0:T(128)}, f32[6]{0:T(128)S(1)}, u32[]{:S(2)}) copy-start(f32[6]{0:T(128)S(1)} %get-tuple-element.23) | copy-start | bytes 76
  9.6 17.9 %copy-start.32 = (s32[6,1]{0,1:T(1,128)}, s32[6,1]{0,1:T(1,128)S(1)}, u32[]{:S(2)}) copy-start(s32[6,1]{0,1:T(1,128)S(1)} %copy.70) | copy-start | bytes 76
  10.1 0.6 copy-start.39
  10.7 56.2 %copy-start.30 = (s32[6]{0:T(128)}, s32[6]{0:T(128)S(1)}, u32[]{:S(2)}) copy-start(s32[6]{0:T(128)S(1)} %fusion.63) | copy-start | bytes 76
  27.4 1.3 copy-start.41
  27.6 58.5 %copy-start.27 = (pred[48]{0:T(512)(128)(4,1)}, pred[48]{0:T(512)(128)(4,1)S(1)}, u32[]{:S(2)}) copy-start(pred[48]{0:T(512)(128)(4,1)S(1)} %ge.28) | copy-start | bytes 148
  30.9 0.9 copy-start.37
  31.9 37.2 %all-to-all-start.1 = ((bf16[16,3,32,128]{3,2,1,0:T(8,128)(2,1)}), bf16[16,3,32,128]{3,2,1,0:T(8,128)(2,1)S(1)}, u32[]{:S(2)}, u32[]{:S(2)}) async-start(bf16[16,3,32,128]{3,2,1,0:T(8,128)(2,1)} %bitcast.8), calls=%async_computation.1 | async-start | bytes 786432 | tf_op jit(solution)/shard_map/all_to_all | solution.py:49
  69.0 110.7 %all-to-all-start.2 = ((f32[16,3,32,128]{3,2,1,0:T(8,128)}), f32[16,3,32,128]{3,2,1,0:T(8,128)}, u32[]{:S(2)}, u32[]{:S(2)}) async-start(f32[16,3,32,128]{3,2,1,0:T(8,128)} %bitcast.95), calls=%async_computation.2 | async-start | bytes 1572864 | tf_op jit(solution)/shard_map/all_to_all | solution.py:74
  76.2 103.6 %all-reduce.5.cloned.1.call-start = ((), (), s32[]{:S(2)}) async-start(), calls=%async_computation.9 | async-start | bytes 1048576 | tf_op jit(solution)/shard_map/psum | solution.py:87
  76.9 7.4 %copy-start.28 = (pred[6]{0:T(512)(128)(4,1)}, pred[6]{0:T(512)(128)(4,1)S(1)}, u32[]{:S(2)}) copy-start(pred[6]{0:T(512)(128)(4,1)S(1)} %get-tuple-element.11) | copy-start | bytes 22
  78.8 6.5 copy-start.14
  78.8 7.2 %copy-start.42 = (s32[48]{0:T(128)S(1)}, s32[48]{0:T(128)}, u32[]{:S(2)}) copy-start(s32[48]{0:T(128)} %get-tuple-element.21) | copy-start | bytes 580
  78.9 100.9 %copy-start.23 = (f32[2,128]{1,0:T(2,128)S(1)}, f32[2,128]{1,0:T(2,128)}, u32[]{:S(2)}) copy-start(f32[2,128]{1,0:T(2,128)} %param.15) | copy-start | bytes 3076
  84.4 146.3 %all-gather.7.cloned.1.call-start = ((), (), s32[]{:S(2)}) async-start(), calls=%async_computation.12 | async-start | bytes 1114112 | tf_op jit(solution)/shard_map/all_gather | solution.py:63
  85.4 97.6 %copy-start.1 = (bf16[3,2,32,128]{3,2,1,0:T(8,128)(2,1)}, bf16[3,2,32,128]{3,2,1,0:T(8,128)(2,1)S(1)}, u32[]{:S(2)}) copy-start(bf16[3,2,32,128]{3,2,1,0:T(8,128)(2,1)S(1)} %slice.43) | copy-start | bytes 147460
  86.1 96.9 %copy-start.33 = (pred[2,48]{1,0:T(4,128)(4,1)}, pred[2,48]{1,0:T(4,128)(4,1)S(1)}, u32[]{:S(2)}) copy-start(pred[2,48]{1,0:T(4,128)(4,1)S(1)} %compare_and_fusion.3) | copy-start | bytes 292
  181.7 0.6 copy-start.5
  186.2 53.2 %all-to-all-start.3 = ((bf16[16,3,32,128]{3,2,1,0:T(8,128)(2,1)}), bf16[16,3,32,128]{3,2,1,0:T(8,128)(2,1)S(1)}, u32[]{:S(2)}, u32[]{:S(2)}) async-start(bf16[16,3,32,128]{3,2,1,0:T(8,128)(2,1)} %bitcast.17), calls=%async_computation.3 | async-start | bytes 786432 | tf_op jit(solution)/shard_map/all_to_all | solution.py:49
  239.4 109.6 %all-to-all-start.4 = ((f32[16,3,32,128]{3,2,1,0:T(8,128)}), f32[16,3,32,128]{3,2,1,0:T(8,128)}, u32[]{:S(2)}, u32[]{:S(2)}) async-start(f32[16,3,32,128]{3,2,1,0:T(8,128)} %bitcast.96), calls=%async_computation.4 | async-start | bytes 1572864 | tf_op jit(solution)/shard_map/all_to_all | solution.py:74
  246.5 102.5 %all-reduce.7.cloned.1.call-start = ((), (), s32[]{:S(2)}) async-start(), calls=%async_computation.11 | async-start | bytes 1048576 | tf_op jit(solution)/shard_map/psum | solution.py:87
  248.1 2.1 copy-start.16
  248.1 2.1 copy-start.20
  248.1 5.6 copy-start.2
  248.1 100.9 %copy-start.13 = (f32[1,2,32,128]{3,2,1,0:T(8,128)S(1)}, f32[1,2,32,128]{3,2,1,0:T(8,128)}, u32[]{:S(2)}) copy-start(f32[1,2,32,128]{3,2,1,0:T(8,128)} %get-tuple-element.17) | copy-start | bytes 98308
  248.1 100.9 %copy-start.24 = (f32[2,128]{1,0:T(2,128)S(1)}, f32[2,128]{1,0:T(2,128)}, u32[]{:S(2)}) copy-start(f32[2,128]{1,0:T(2,128)} %param.15) | copy-start | bytes 3076
  248.1 100.9 %copy-start.34 = (pred[2,48]{1,0:T(4,128)(4,1)S(1)}, pred[2,48]{1,0:T(4,128)(4,1)}, u32[]{:S(2)}) copy-start(pred[2,48]{1,0:T(4,128)(4,1)} %copy-done.33) | copy-start | bytes 292
  253.7 146.3 %all-gather.9.cloned.1.call-start = ((), (), s32[]{:S(2)}) async-start(), calls=%async_computation.14 | async-start | bytes 1114112 | tf_op jit(solution)/shard_map/all_gather | solution.py:63
  253.7 98.5 %copy-start.3 = (bf16[3,2,32,128]{3,2,1,0:T(8,128)(2,1)}, bf16[3,2,32,128]{3,2,1,0:T(8,128)(2,1)S(1)}, u32[]{:S(2)}) copy-start(bf16[3,2,32,128]{3,2,1,0:T(8,128)(2,1)S(1)} %fusion.39) | copy-start | bytes 147460
  350.9 0.6 copy-start.7
  355.4 53.2 %all-to-all-start.5 = ((bf16[16,3,32,128]{3,2,1,0:T(8,128)(2,1)}), bf16[16,3,32,128]{3,2,1,0:T(8,128)(2,1)S(1)}, u32[]{:S(2)}, u32[]{:S(2)}) async-start(bf16[16,3,32,128]{3,2,1,0:T(8,128)(2,1)} %bitcast.25), calls=%async_computation.5 | async-start | bytes 786432 | tf_op jit(solution)/shard_map/all_to_all | solution.py:49
  408.6 109.5 %all-to-all-start.6 = ((f32[16,3,32,128]{3,2,1,0:T(8,128)}), f32[16,3,32,128]{3,2,1,0:T(8,128)}, u32[]{:S(2)}, u32[]{:S(2)}) async-start(f32[16,3,32,128]{3,2,1,0:T(8,128)} %bitcast.97), calls=%async_computation.6 | async-start | bytes 1572864 | tf_op jit(solution)/shard_map/all_to_all | solution.py:74
  415.8 102.3 %all-reduce.9.cloned.1.call-start = ((), (), s32[]{:S(2)}) async-start(), calls=%async_computation.13 | async-start | bytes 1048576 | tf_op jit(solution)/shard_map/psum | solution.py:87
  417.1 2.1 copy-start.17
  417.1 2.1 copy-start.21
  417.1 5.6 copy-start.4
  417.1 100.9 %copy-start.12 = (f32[1,2,32,128]{3,2,1,0:T(8,128)S(1)}, f32[1,2,32,128]{3,2,1,0:T(8,128)}, u32[]{:S(2)}) copy-start(f32[1,2,32,128]{3,2,1,0:T(8,128)} %get-tuple-element.16) | copy-start | bytes 98308
  417.1 100.9 %copy-start.25 = (f32[2,128]{1,0:T(2,128)S(1)}, f32[2,128]{1,0:T(2,128)}, u32[]{:S(2)}) copy-start(f32[2,128]{1,0:T(2,128)} %param.15) | copy-start | bytes 3076
  417.1 100.9 %copy-start.35 = (pred[2,48]{1,0:T(4,128)(4,1)S(1)}, pred[2,48]{1,0:T(4,128)(4,1)}, u32[]{:S(2)}) copy-start(pred[2,48]{1,0:T(4,128)(4,1)} %copy-done.33) | copy-start | bytes 292
  422.7 146.3 %all-gather.11.cloned.1.call-start = ((), (), s32[]{:S(2)}) async-start(), calls=%async_computation.16 | async-start | bytes 1114112 | tf_op jit(solution)/shard_map/all_gather | solution.py:63
  520.0 0.6 copy-start.9
  524.5 53.1 %all-to-all-start.7 = ((bf16[16,3,32,128]{3,2,1,0:T(8,128)(2,1)}), bf16[16,3,32,128]{3,2,1,0:T(8,128)(2,1)S(1)}, u32[]{:S(2)}, u32[]{:S(2)}) async-start(bf16[16,3,32,128]{3,2,1,0:T(8,128)(2,1)} %bitcast.33), calls=%async_computation.7 | async-start | bytes 786432 | tf_op jit(solution)/shard_map/all_to_all | solution.py:49
  569.1 6.3 copy-start.31
  571.9 14.4 %copy-start.29 = (pred[6]{0:T(512)(128)(4,1)S(1)}, pred[6]{0:T(512)(128)(4,1)}, u32[]{:S(2)}) copy-start(pred[6]{0:T(512)(128)(4,1)} %copy-done.28) | copy-start | bytes 22
  577.6 10.8 %copy-start.18 = (f32[6]{0:T(128)S(1)}, f32[6]{0:T(128)}, u32[]{:S(2)}) copy-start(f32[6]{0:T(128)} %copy-done.15) | copy-start | bytes 76
  577.6 10.8 %copy-start.22 = (s32[6]{0:T(128)S(1)}, s32[6]{0:T(128)}, u32[]{:S(2)}) copy-start(s32[6]{0:T(128)} %copy-done.19) | copy-start | bytes 76
  577.6 109.7 %all-to-all-start.8 = ((f32[16,3,32,128]{3,2,1,0:T(8,128)}), f32[16,3,32,128]{3,2,1,0:T(8,128)}, u32[]{:S(2)}, u32[]{:S(2)}) async-start(f32[16,3,32,128]{3,2,1,0:T(8,128)} %bitcast.94), calls=%async_computation.8 | async-start | bytes 1572864 | tf_op jit(solution)/shard_map/all_to_all | solution.py:74
  584.7 102.5 %all-reduce.11.cloned.1.call-start = ((), (), s32[]{:S(2)}) async-start(), calls=%async_computation.15 | async-start | bytes 1048576 | tf_op jit(solution)/shard_map/psum | solution.py:87
  586.3 100.9 %copy-start.11 = (f32[1,2,32,128]{3,2,1,0:T(8,128)S(1)}, f32[1,2,32,128]{3,2,1,0:T(8,128)}, u32[]{:S(2)}) copy-start(f32[1,2,32,128]{3,2,1,0:T(8,128)} %get-tuple-element.15) | copy-start | bytes 98308
  586.3 100.9 %copy-start.26 = (f32[2,128]{1,0:T(2,128)S(1)}, f32[2,128]{1,0:T(2,128)}, u32[]{:S(2)}) copy-start(f32[2,128]{1,0:T(2,128)} %param.15) | copy-start | bytes 3076
  586.3 100.9 %copy-start.36 = (pred[2,48]{1,0:T(4,128)(4,1)S(1)}, pred[2,48]{1,0:T(4,128)(4,1)}, u32[]{:S(2)}) copy-start(pred[2,48]{1,0:T(4,128)(4,1)} %copy-done.33) | copy-start | bytes 292
  588.4 100.8 %copy-start.6 = (f32[1,2,32,128]{3,1,2,0:T(2,128)S(1)}, f32[1,2,32,128]{3,1,2,0:T(2,128)}, u32[]{:S(2)}) copy-start(f32[1,2,32,128]{3,1,2,0:T(2,128)} %copy-done.5) | copy-start | bytes 98308
  588.4 100.8 %copy-start.8 = (f32[1,2,32,128]{3,1,2,0:T(2,128)S(1)}, f32[1,2,32,128]{3,1,2,0:T(2,128)}, u32[]{:S(2)}) copy-start(f32[1,2,32,128]{3,1,2,0:T(2,128)} %copy-done.7) | copy-start | bytes 98308
  588.4 100.8 %copy-start.10 = (f32[1,2,32,128]{3,1,2,0:T(2,128)S(1)}, f32[1,2,32,128]{3,1,2,0:T(2,128)}, u32[]{:S(2)}) copy-start(f32[1,2,32,128]{3,1,2,0:T(2,128)} %copy-done.9) | copy-start | bytes 98308
Sparse Core Ops, SparseCore 0:
  9.7 50.7 all-gather.4
  84.5 95.1 all-reduce.4
  183.1 47.6 all-gather.6
  253.8 95.1 all-reduce.6
  352.3 47.6 all-gather.8
  422.8 95.1 all-reduce.8
  521.4 47.6 all-gather.10
  592.0 95.1 all-reduce.10
where the time goes:
time: 699 us; the launch traced here: 697 us
  waiting for transfers between devices  515 us (74%)
  starting transfers between devices  54.3 us (8%)
  local copies, waits for them, and re-layouts  41.9 us (6%)
  matrix products  39.5 us (6%)
  blocking collectives  16 us (2%)
  other arithmetic  15.7 us (2%)
  between operations  14 us (2%)
    psum x4, waiting for transfers between devices, shards(): total = lax.psum(forward_sum, 'cols')  380 us
    all_gather x4, waiting for transfers between devices, shards(): collected = lax.all_gather(rounded, 'cols', axis=3, tiled=True)  136 us
    all_to_all x4, starting transfers between devices, shards(): lax.all_to_all(outbound.reshape(groups, SM, excite, width), 'pairs', spli...  28.7 us
    all_to_all x4, starting transfers between devices, shards(): lax.all_to_all(outgoing.reshape(groups, SM, excite, width), 'pairs', spli...  24.9 us
    all_to_all x1, blocking collectives, shards(): lax.all_to_all(codes.reshape(groups, SM), 'pairs', split_axis=0, concat_a...  16 us
  transfers between devices with their start and end apart: 16, of which 8 were waited for; matrix products, arithmetic and copies ran while one was open for 12% of the time, Pallas kernels for 0%

commit v1 on v0

--- a/solution.py
+++ b/solution.py
@@ -84,7 +84,8 @@
             received.reshape(buffer_rows, excite, width),
             precision=lax.Precision.HIGHEST,
         )
-        total = lax.psum(forward_sum, "cols")
+        pieces = lax.all_gather(forward_sum, "cols", axis=0, tiled=False)
+        total = pieces.sum(axis=0)
         own_part = lax.dynamic_slice_in_dim(total, lax.axis_index("cols") * width, width, 2)
         field = own_part + backward_sum
         fresh = (excitation[step] - field) / diagonal[:, None, :]

time: 699 us -> 570 us (0.82)
  waiting for transfers between devices: 515 us -> 338 us
  blocking collectives: 16 us -> 61.7 us
  other arithmetic: 15.7 us -> 29.8 us
  starting transfers between devices: 54.3 us -> 41.2 us
    psum x4 -> x0, waiting for transfers between devices: 380 us -> none  [shards(): total = lax.psum(forward_sum, 'cols')]
    all_gather x0 -> x4, waiting for transfers between devices: none -> 251 us  [shards(): pieces = lax.all_gather(forward_sum, 'cols', axis=0, tiled=False)]
    all_gather x4, waiting for transfers between devices: 136 us -> 69.4 us  [shards(): collected = lax.all_gather(rounded, 'cols', axis=3, tiled=True)]
    all_to_all x1 -> x3, blocking collectives: 16 us -> 61.7 us  [shards(): lax.all_to_all(outgoing.reshape(groups, SM, excite, width), 'pairs', spli...]
    all_to_all x4 -> x1, starting transfers between devices: 24.9 us -> 3.55 us  [shards(): lax.all_to_all(outgoing.reshape(groups, SM, excite, width), 'pairs', spli...]
    reduce_sum x0 -> x4, other arithmetic: none -> 18.9 us  [shards(): total = pieces.sum(axis=0)]
    all_to_all x4 -> x1, waiting for transfers between devices: 0.01 us -> 12.2 us  [shards(): lax.all_to_all(outgoing.reshape(groups, SM, excite, width), 'pairs', spli...]
    all_to_all x0 -> x1, starting transfers between devices: none -> 8.57 us  [shards(): lax.all_to_all(codes.reshape(groups, SM), 'pairs', split_axis=0, concat_a...]
  transfers between devices with their start and end apart: 16 -> 14, of which waited for: 8 -> 10; matrix products, arithmetic and copies ran while one was open for 12% -> 17% of each run, Pallas kernels for 0% -> 0%
where the time goes in v1:
time: 570 us; the launch traced here: 567 us
  waiting for transfers between devices  338 us (59%)
  blocking collectives  61.7 us (11%)
  local copies, waits for them, and re-layouts  48.3 us (8%)
  starting transfers between devices  41.2 us (7%)
  matrix products  33.6 us (6%)
  other arithmetic  29.8 us (5%)
  between operations  14.2 us (2%)
    all_gather x4, waiting for transfers between devices, shards(): pieces = lax.all_gather(forward_sum, 'cols', axis=0, tiled=False)  251 us
    all_gather x4, waiting for transfers between devices, shards(): collected = lax.all_gather(rounded, 'cols', axis=3, tiled=True)  69.4 us
    all_to_all x3, blocking collectives, shards(): lax.all_to_all(outgoing.reshape(groups, SM, excite, width), 'pairs', spli...  61.7 us
    all_to_all x4, starting transfers between devices, shards(): lax.all_to_all(outbound.reshape(groups, SM, excite, width), 'pairs', spli...  28.5 us
    reduce_sum x4, other arithmetic, shards(): total = pieces.sum(axis=0)  18.9 us
    all_to_all x1, waiting for transfers between devices, shards(): lax.all_to_all(outgoing.reshape(groups, SM, excite, width), 'pairs', spli...  12.2 us
  transfers between devices with their start and end apart: 14, of which 10 were waited for; matrix products, arithmetic and copies ran while one was open for 17% of the time, Pallas kernels for 0%

profile of v1, /device:TPU:2, one launch (start us, length us, event | category | flops | bytes accessed | tf_op | source)
XLA Modules:
  0.0 567.0 jit_solution(7948942046672317914)
XLA Ops:
  6.5 1.1 slice_reduce_fusion
  9.5 8.6 %all-to-all-start = ((s32[16,1,3]{2,1,0:T(1,128)}), s32[16,1,3]{2,1,0:T(1,128)S(1)}, u32[]{:S(2)}, u32[]{:S(2)}) async-start(s32[16,1,3]{2,1,0:T(1,128)} %bitcast.6), calls=%async_computation | async-start | bytes 16384 | tf_op jit(solution)/shard_map/all_to_all | solution.py:27
  18.1 1.5 convert_element_type.42
  19.7 6.0 %all-to-all-done = s32[16,1,3]{2,1,0:T(1,128)S(1)} async-done(((s32[16,1,3]{2,1,0:T(1,128)}), s32[16,1,3]{2,1,0:T(1,128)S(1)}, u32[]{:S(2)}, u32[]{:S(2)}) %all-to-all-start) | async-done | bytes 224 | tf_op jit(solution)/shard_map/all_to_all | solution.py:27
  26.6 1.5 gather_fusion
  29.7 3.6 all-to-all-start.1
  34.6 12.2 %all-to-all-done.1 = bf16[16,3,32,128]{3,2,1,0:T(8,128)(2,1)S(1)} async-done(((bf16[16,3,32,128]{3,2,1,0:T(8,128)(2,1)}), bf16[16,3,32,128]{3,2,1,0:T(8,128)(2,1)S(1)}, u32[]{:S(2)}, u32[]{:S(2)}) %all-to-all-start.1) | async-done | bytes 393248 | tf_op jit(solution)/shard_map/all_to_all | solution.py:49
  46.8 1.3 gather_fusion.1
  48.1 2.0 fusion.46
  50.0 2.7 fusion.6
  52.8 1.1 copy.85
  54.0 16.8 %all-gather.13.cloned.1.call-done = bf16[4,2,32,2048]{3,2,1,0:T(8,128)(2,1)} async-done(((bf16[4,2,32,128]{3,2,1,0:T(8,128)(2,1)}), bf16[4,2,32,2048]{3,2,1,0:T(8,128)(2,1)}) %all-gather.13.cloned.1.call-update) | async-done | bytes 1048592 | tf_op jit(solution)/shard_map/all_gather | solution.py:63
  70.7 2.7 gather_fusion.2
  73.5 1.8 convolution_multiply_fusion.3
  75.3 1.0 broadcast.143.clone
  76.3 2.1 scatter_fusion
  78.4 7.1 %all-to-all-start.2 = ((f32[16,3,32,128]{3,2,1,0:T(8,128)}), f32[16,3,32,128]{3,2,1,0:T(8,128)}, u32[]{:S(2)}, u32[]{:S(2)}) async-start(f32[16,3,32,128]{3,2,1,0:T(8,128)} %bitcast.103), calls=%async_computation.2 | async-start | bytes 1572864 | tf_op jit(solution)/shard_map/all_to_all | solution.py:74
  87.2 61.6 %all-gather.21.cloned.1.call-done = f32[32,32,2048]{2,1,0:T(8,128)} async-done(((f32[2,32,2048]{2,1,0:T(8,128)}), f32[32,32,2048]{2,1,0:T(8,128)}) %all-gather.21.cloned.1.call-update) | async-done | bytes 8388624 | tf_op jit(solution)/shard_map/all_gather | solution.py:87
  148.8 4.7 reduce_sum.46
  154.3 1.9 fusion.19
  157.5 1.6 gather_fusion.3
  159.9 20.6 %all_to_all.49 = bf16[16,3,32,128]{3,2,1,0:T(8,128)(2,1)S(1)} all-to-all(bf16[16,3,32,128]{3,2,1,0:T(8,128)(2,1)S(1)} %bitcast.107), channel_id=1, replica_groups=mesh['pairs'=16,'cols'=16] {'pairs'}, dimensions={0} | all-to-all | bytes 786432 | tf_op jit(solution)/shard_map/all_to_all | solution.py:49
  180.5 1.3 gather_fusion.4
  181.8 2.0 fusion.44
  183.8 2.7 fusion.4
  186.5 1.1 copy.91
  187.6 17.6 %all-gather.15.cloned.1.call-done = bf16[4,2,32,2048]{3,2,1,0:T(8,128)(2,1)} async-done(((bf16[4,2,32,128]{3,2,1,0:T(8,128)(2,1)}), bf16[4,2,32,2048]{3,2,1,0:T(8,128)(2,1)}) %all-gather.15.cloned.1.call-update) | async-done | bytes 1048592 | tf_op jit(solution)/shard_map/all_gather | solution.py:63
  205.2 2.9 gather_fusion.5
  208.1 1.8 convolution_multiply_fusion.2
  209.9 1.0 broadcast.143.clone.1
  210.9 2.1 scatter_fusion.1
  212.9 7.1 %all-to-all-start.4 = ((f32[16,3,32,128]{3,2,1,0:T(8,128)}), f32[16,3,32,128]{3,2,1,0:T(8,128)}, u32[]{:S(2)}, u32[]{:S(2)}) async-start(f32[16,3,32,128]{3,2,1,0:T(8,128)} %bitcast.104), calls=%async_computation.4 | async-start | bytes 1572864 | tf_op jit(solution)/shard_map/all_to_all | solution.py:74
  220.1 63.0 %all-gather.23.cloned.1.call-done = f32[32,32,2048]{2,1,0:T(8,128)} async-done(((f32[2,32,2048]{2,1,0:T(8,128)}), f32[32,32,2048]{2,1,0:T(8,128)}) %all-gather.23.cloned.1.call-update) | async-done | bytes 8388624 | tf_op jit(solution)/shard_map/all_gather | solution.py:87
  283.1 4.7 reduce_sum.47
  288.6 1.9 fusion.16
  291.9 1.6 gather_fusion.6
  294.3 20.6 %all_to_all.50 = bf16[16,3,32,128]{3,2,1,0:T(8,128)(2,1)S(1)} all-to-all(bf16[16,3,32,128]{3,2,1,0:T(8,128)(2,1)S(1)} %bitcast.108), channel_id=1, replica_groups=mesh['pairs'=16,'cols'=16] {'pairs'}, dimensions={0} | all-to-all | bytes 786432 | tf_op jit(solution)/shard_map/all_to_all | solution.py:49
  314.8 1.3 gather_fusion.7
  316.1 2.0 fusion.42
  318.1 2.7 fusion.2
  320.8 1.1 copy.97
  322.0 17.6 %all-gather.17.cloned.1.call-done = bf16[4,2,32,2048]{3,2,1,0:T(8,128)(2,1)} async-done(((bf16[4,2,32,128]{3,2,1,0:T(8,128)(2,1)}), bf16[4,2,32,2048]{3,2,1,0:T(8,128)(2,1)}) %all-gather.17.cloned.1.call-update) | async-done | bytes 1048592 | tf_op jit(solution)/shard_map/all_gather | solution.py:63
  339.5 2.9 gather_fusion.8
  342.4 1.8 convolution_multiply_fusion.1
  345.2 2.1 scatter_fusion.2
  347.3 7.1 %all-to-all-start.6 = ((f32[16,3,32,128]{3,2,1,0:T(8,128)}), f32[16,3,32,128]{3,2,1,0:T(8,128)}, u32[]{:S(2)}, u32[]{:S(2)}) async-start(f32[16,3,32,128]{3,2,1,0:T(8,128)} %bitcast.105), calls=%async_computation.6 | async-start | bytes 1572864 | tf_op jit(solution)/shard_map/all_to_all | solution.py:74
  354.7 62.8 %all-gather.25.cloned.1.call-done = f32[32,32,2048]{2,1,0:T(8,128)} async-done(((f32[2,32,2048]{2,1,0:T(8,128)}), f32[32,32,2048]{2,1,0:T(8,128)}) %all-gather.25.cloned.1.call-update) | async-done | bytes 8388624 | tf_op jit(solution)/shard_map/all_gather | solution.py:87
  417.4 4.7 reduce_sum.48
  423.0 1.9 fusion.13
  426.2 1.6 gather_fusion.9
  428.6 20.6 %all_to_all.51 = bf16[16,3,32,128]{3,2,1,0:T(8,128)(2,1)S(1)} all-to-all(bf16[16,3,32,128]{3,2,1,0:T(8,128)(2,1)S(1)} %bitcast.106), channel_id=1, replica_groups=mesh['pairs'=16,'cols'=16] {'pairs'}, dimensions={0} | all-to-all | bytes 786432 | tf_op jit(solution)/shard_map/all_to_all | solution.py:49
  449.2 1.3 gather_fusion.10
  450.5 2.0 fusion.40
  452.5 2.7 fusion
  455.2 1.1 copy.103
  456.3 17.5 %all-gather.19.cloned.1.call-done = bf16[4,2,32,2048]{3,2,1,0:T(8,128)(2,1)} async-done(((bf16[4,2,32,128]{3,2,1,0:T(8,128)(2,1)}), bf16[4,2,32,2048]{3,2,1,0:T(8,128)(2,1)}) %all-gather.19.cloned.1.call-update) | async-done | bytes 1048592 | tf_op jit(solution)/shard_map/all_gather | solution.py:63
  473.9 2.9 gather_fusion.11
  476.7 1.8 convolution_multiply_fusion
  478.5 1.0 broadcast.143
  479.5 2.1 scatter_fusion.3
  481.6 7.1 %all-to-all-start.8 = ((f32[16,3,32,128]{3,2,1,0:T(8,128)}), f32[16,3,32,128]{3,2,1,0:T(8,128)}, u32[]{:S(2)}, u32[]{:S(2)}) async-start(f32[16,3,32,128]{3,2,1,0:T(8,128)} %bitcast.102), calls=%async_computation.8 | async-start | bytes 1572864 | tf_op jit(solution)/shard_map/all_to_all | solution.py:74
  488.7 63.2 %all-gather.27.cloned.1.call-done = f32[32,32,2048]{2,1,0:T(8,128)} async-done(((f32[2,32,2048]{2,1,0:T(8,128)}), f32[32,32,2048]{2,1,0:T(8,128)}) %all-gather.27.cloned.1.call-update) | async-done | bytes 8388624 | tf_op jit(solution)/shard_map/all_gather | solution.py:87
  551.9 4.7 reduce_sum.49
  557.4 1.9 fusion.10
  (167 shorter events, 18.9 us)
Async XLA Ops:
  6.5 41.5 %copy-start = (bf16[6,2048,128]{2,1,0:T(8,128)(2,1)S(1)}, bf16[6,2048,128]{2,1,0:T(8,128)(2,1)}, u32[]{:S(2)}) copy-start(bf16[6,2048,128]{2,1,0:T(8,128)(2,1)} %param.12) | copy-start | bytes 9437188
  7.7 18.9 %copy-start.48 = (s32[6]{0:T(128)}, s32[6]{0:T(128)S(1)}, u32[]{:S(2)}) copy-start(s32[6]{0:T(128)S(1)} %get-tuple-element.10) | copy-start | bytes 76
  7.7 46.2 %copy-start.19 = (s32[6]{0:T(128)}, s32[6]{0:T(128)S(1)}, u32[]{:S(2)}) copy-start(s32[6]{0:T(128)S(1)} %get-tuple-element.8) | copy-start | bytes 76
  7.8 11.9 %copy-start.46 = (s32[6,1]{0,1:T(1,128)}, s32[6,1]{0,1:T(1,128)S(1)}, u32[]{:S(2)}) copy-start(s32[6,1]{0,1:T(1,128)S(1)} %copy.108) | copy-start | bytes 76
  7.8 65.7 %copy-start.15 = (f32[6]{0:T(128)}, f32[6]{0:T(128)S(1)}, u32[]{:S(2)}) copy-start(f32[6]{0:T(128)S(1)} %get-tuple-element.23) | copy-start | bytes 76
  7.9 11.8 %copy-start.38 = (s32[6,1]{0,1:T(1,128)}, s32[6,1]{0,1:T(1,128)S(1)}, u32[]{:S(2)}) copy-start(s32[6,1]{0,1:T(1,128)S(1)} %copy.109) | copy-start | bytes 76
  8.2 18.4 %copy-start.47 = (s32[6]{0:T(128)}, s32[6]{0:T(128)S(1)}, u32[]{:S(2)}) copy-start(s32[6]{0:T(128)S(1)} %select_reduce_fusion) | copy-start | bytes 76
  8.2 1.3 copy-start.29
  9.5 16.2 %all-to-all-start = ((s32[16,1,3]{2,1,0:T(1,128)}), s32[16,1,3]{2,1,0:T(1,128)S(1)}, u32[]{:S(2)}, u32[]{:S(2)}) async-start(s32[16,1,3]{2,1,0:T(1,128)} %bitcast.6), calls=%async_computation | async-start | bytes 16384 | tf_op jit(solution)/shard_map/all_to_all | solution.py:27
  18.1 52.7 %all-gather.13.cloned.1.call-start = ((), (), s32[]{:S(2)}) async-start(), calls=%async_computation.9 | async-start | bytes 1114112 | tf_op jit(solution)/shard_map/all_gather | solution.py:63
  25.8 0.8 copy-start.50
  26.5 60.6 %copy-start.26 = (pred[48]{0:T(512)(128)(4,1)}, pred[48]{0:T(512)(128)(4,1)S(1)}, u32[]{:S(2)}) copy-start(pred[48]{0:T(512)(128)(4,1)S(1)} %ge.28) | copy-start | bytes 148
  26.6 6.7 %copy-start.40 = (s32[1024]{0:T(1024)}, s32[1024]{0:T(1024)S(1)}, u32[]{:S(2)}) copy-start(s32[1024]{0:T(1024)S(1)} %pad_clamp_fusion.2) | copy-start | bytes 12292
  28.8 0.9 copy-start.41
  29.7 17.1 %all-to-all-start.1 = ((bf16[16,3,32,128]{3,2,1,0:T(8,128)(2,1)}), bf16[16,3,32,128]{3,2,1,0:T(8,128)(2,1)S(1)}, u32[]{:S(2)}, u32[]{:S(2)}) async-start(bf16[16,3,32,128]{3,2,1,0:T(8,128)(2,1)} %bitcast.8), calls=%async_computation.1 | async-start | bytes 786432 | tf_op jit(solution)/shard_map/all_to_all | solution.py:49
  33.2 115.5 %all-gather.21.cloned.1.call-start = ((), (), s32[]{:S(2)}) async-start(), calls=%async_computation.13 | async-start | bytes 8912896 | tf_op jit(solution)/shard_map/all_gather | solution.py:87
  34.0 18.8 %copy-start.28 = (pred[6]{0:T(512)(128)(4,1)}, pred[6]{0:T(512)(128)(4,1)S(1)}, u32[]{:S(2)}) copy-start(pred[6]{0:T(512)(128)(4,1)S(1)} %get-tuple-element.11) | copy-start | bytes 22
  50.0 3.9 copy-start.49
  53.9 22.4 %copy-start.34 = (pred[6]{0:T(512)(128)(4,1)}, pred[6]{0:T(512)(128)(4,1)S(1)}, u32[]{:S(2)}) copy-start(pred[6]{0:T(512)(128)(4,1)S(1)} %get-tuple-element.13) | copy-start | bytes 22
  54.0 22.3 %copy-start.39 = (s32[1024]{0:T(1024)}, s32[1024]{0:T(1024)S(1)}, u32[]{:S(2)}) copy-start(s32[1024]{0:T(1024)S(1)} %pad_clamp_fusion) | copy-start | bytes 12292
  70.7 5.6 copy-start.30
  73.5 13.0 %copy-start.11 = (f32[4,2,32,128]{3,2,1,0:T(8,128)S(1)}, f32[4,2,32,128]{3,2,1,0:T(8,128)}, u32[]{:S(2)}) copy-start(f32[4,2,32,128]{3,2,1,0:T(8,128)} %param.14) | copy-start | bytes 393220
  73.5 13.7 %copy-start.51 = (s32[48]{0:T(128)S(1)}, s32[48]{0:T(128)}, u32[]{:S(2)}) copy-start(s32[48]{0:T(128)} %get-tuple-element.21) | copy-start | bytes 580
  78.4 75.9 %all-to-all-start.2 = ((f32[16,3,32,128]{3,2,1,0:T(8,128)}), f32[16,3,32,128]{3,2,1,0:T(8,128)}, u32[]{:S(2)}, u32[]{:S(2)}) async-start(f32[16,3,32,128]{3,2,1,0:T(8,128)} %bitcast.103), calls=%async_computation.2 | async-start | bytes 1572864 | tf_op jit(solution)/shard_map/all_to_all | solution.py:74
  85.5 119.7 %all-gather.15.cloned.1.call-start = ((), (), s32[]{:S(2)}) async-start(), calls=%async_computation.10 | async-start | bytes 1114112 | tf_op jit(solution)/shard_map/all_gather | solution.py:63
  86.5 70.3 %copy-start.1 = (bf16[3,2,32,128]{3,2,1,0:T(8,128)(2,1)}, bf16[3,2,32,128]{3,2,1,0:T(8,128)(2,1)S(1)}, u32[]{:S(2)}) copy-start(bf16[3,2,32,128]{3,2,1,0:T(8,128)(2,1)S(1)} %slice.43) | copy-start | bytes 147460
  87.2 67.1 %copy-start.42 = (pred[2,48]{1,0:T(4,128)(4,1)}, pred[2,48]{1,0:T(4,128)(4,1)S(1)}, u32[]{:S(2)}) copy-start(pred[2,48]{1,0:T(4,128)(4,1)S(1)} %compare_and_fusion.3) | copy-start | bytes 292
  148.8 5.5 copy-start.23
  156.2 0.6 copy-start.5
  157.5 125.6 %all-gather.23.cloned.1.call-start = ((), (), s32[]{:S(2)}) async-start(), calls=%async_computation.14 | async-start | bytes 8912896 | tf_op jit(solution)/shard_map/all_gather | solution.py:87
  181.8 2.0 copy-start.16
  181.8 2.0 copy-start.20
  183.8 24.3 %copy-start.35 = (pred[6]{0:T(512)(128)(4,1)S(1)}, pred[6]{0:T(512)(128)(4,1)}, u32[]{:S(2)}) copy-start(pred[6]{0:T(512)(128)(4,1)} %copy-done.34) | copy-start | bytes 22
  205.2 5.7 copy-start.31
  208.1 12.0 %copy-start.2 = (bf16[3,2,32,128]{3,2,1,0:T(8,128)(2,1)S(1)}, bf16[3,2,32,128]{3,2,1,0:T(8,128)(2,1)}, u32[]{:S(2)}) copy-start(bf16[3,2,32,128]{3,2,1,0:T(8,128)(2,1)} %copy-done.1) | copy-start | bytes 147460
  212.9 75.7 %all-to-all-start.4 = ((f32[16,3,32,128]{3,2,1,0:T(8,128)}), f32[16,3,32,128]{3,2,1,0:T(8,128)}, u32[]{:S(2)}, u32[]{:S(2)}) async-start(f32[16,3,32,128]{3,2,1,0:T(8,128)} %bitcast.104), calls=%async_computation.4 | async-start | bytes 1572864 | tf_op jit(solution)/shard_map/all_to_all | solution.py:74
  220.1 119.5 %all-gather.17.cloned.1.call-start = ((), (), s32[]{:S(2)}) async-start(), calls=%async_computation.11 | async-start | bytes 1114112 | tf_op jit(solution)/shard_map/all_gather | solution.py:63
  220.1 71.0 %copy-start.3 = (bf16[3,2,32,128]{3,2,1,0:T(8,128)(2,1)}, bf16[3,2,32,128]{3,2,1,0:T(8,128)(2,1)S(1)}, u32[]{:S(2)}) copy-start(bf16[3,2,32,128]{3,2,1,0:T(8,128)(2,1)S(1)} %fusion.39) | copy-start | bytes 147460
  283.1 5.5 copy-start.14
  283.1 5.5 copy-start.24
  283.1 5.5 copy-start.43
  291.8 125.6 %all-gather.25.cloned.1.call-start = ((), (), s32[]{:S(2)}) async-start(), calls=%async_computation.15 | async-start | bytes 8912896 | tf_op jit(solution)/shard_map/all_gather | solution.py:87
  316.1 2.0 copy-start.17
  316.1 2.0 copy-start.21
  318.1 24.3 %copy-start.36 = (pred[6]{0:T(512)(128)(4,1)S(1)}, pred[6]{0:T(512)(128)(4,1)}, u32[]{:S(2)}) copy-start(pred[6]{0:T(512)(128)(4,1)} %copy-done.34) | copy-start | bytes 22
  339.5 5.7 %copy-start.32 = (s32[6]{0:T(128)S(1)}, s32[6]{0:T(128)}, u32[]{:S(2)}) copy-start(s32[6]{0:T(128)} %copy-done.29) | copy-start | bytes 76
  342.4 12.3 %copy-start.4 = (bf16[3,2,32,128]{3,2,1,0:T(8,128)(2,1)S(1)}, bf16[3,2,32,128]{3,2,1,0:T(8,128)(2,1)}, u32[]{:S(2)}) copy-start(bf16[3,2,32,128]{3,2,1,0:T(8,128)(2,1)} %copy-done.3) | copy-start | bytes 147460
  347.3 75.7 %all-to-all-start.6 = ((f32[16,3,32,128]{3,2,1,0:T(8,128)}), f32[16,3,32,128]{3,2,1,0:T(8,128)}, u32[]{:S(2)}, u32[]{:S(2)}) async-start(f32[16,3,32,128]{3,2,1,0:T(8,128)} %bitcast.105), calls=%async_computation.6 | async-start | bytes 1572864 | tf_op jit(solution)/shard_map/all_to_all | solution.py:74
  354.4 119.5 %all-gather.19.cloned.1.call-start = ((), (), s32[]{:S(2)}) async-start(), calls=%async_computation.12 | async-start | bytes 1114112 | tf_op jit(solution)/shard_map/all_gather | solution.py:63
  417.4 5.5 copy-start.13
  417.4 5.5 copy-start.25
  417.4 5.5 copy-start.44
  417.4 10.3 %copy-start.27 = (pred[48]{0:T(512)(128)(4,1)S(1)}, pred[48]{0:T(512)(128)(4,1)}, u32[]{:S(2)}) copy-start(pred[48]{0:T(512)(128)(4,1)} %copy-done.26) | copy-start | bytes 148
  426.1 125.8 %all-gather.27.cloned.1.call-start = ((), (), s32[]{:S(2)}) async-start(), calls=%async_computation.16 | async-start | bytes 8912896 | tf_op jit(solution)/shard_map/all_gather | solution.py:87
  427.8 24.7 %copy-start.18 = (f32[6]{0:T(128)S(1)}, f32[6]{0:T(128)}, u32[]{:S(2)}) copy-start(f32[6]{0:T(128)} %copy-done.15) | copy-start | bytes 76
  427.8 24.7 %copy-start.22 = (s32[6]{0:T(128)S(1)}, s32[6]{0:T(128)}, u32[]{:S(2)}) copy-start(s32[6]{0:T(128)} %copy-done.19) | copy-start | bytes 76
  452.5 24.3 %copy-start.37 = (pred[6]{0:T(512)(128)(4,1)S(1)}, pred[6]{0:T(512)(128)(4,1)}, u32[]{:S(2)}) copy-start(pred[6]{0:T(512)(128)(4,1)} %copy-done.34) | copy-start | bytes 22
  473.9 5.7 copy-start.33
  481.6 75.9 %all-to-all-start.8 = ((f32[16,3,32,128]{3,2,1,0:T(8,128)}), f32[16,3,32,128]{3,2,1,0:T(8,128)}, u32[]{:S(2)}, u32[]{:S(2)}) async-start(f32[16,3,32,128]{3,2,1,0:T(8,128)} %bitcast.102), calls=%async_computation.8 | async-start | bytes 1572864 | tf_op jit(solution)/shard_map/all_to_all | solution.py:74
  551.9 5.5 copy-start.12
  551.9 5.5 copy-start.45
  551.9 7.4 %copy-start.6 = (f32[1,2,32,128]{3,1,2,0:T(2,128)S(1)}, f32[1,2,32,128]{3,1,2,0:T(2,128)}, u32[]{:S(2)}) copy-start(f32[1,2,32,128]{3,1,2,0:T(2,128)} %copy-done.5) | copy-start | bytes 98308
  551.9 7.5 %copy-start.8 = (f32[1,2,32,128]{3,1,2,0:T(2,128)S(1)}, f32[1,2,32,128]{3,1,2,0:T(2,128)}, u32[]{:S(2)}) copy-start(f32[1,2,32,128]{3,1,2,0:T(2,128)} %copy-done.7) | copy-start | bytes 98308
  551.9 7.5 %copy-start.10 = (f32[1,2,32,128]{3,1,2,0:T(2,128)S(1)}, f32[1,2,32,128]{3,1,2,0:T(2,128)}, u32[]{:S(2)}) copy-start(f32[1,2,32,128]{3,1,2,0:T(2,128)} %copy-done.9) | copy-start | bytes 98308
  (2 other events, 1.2 us)
Sparse Core Ops, SparseCore 0:
  21.3 49.4 all-gather.12
  73.2 75.5 all-gather.20
  157.6 47.5 all-gather.14
  207.5 75.5 all-gather.22
  291.9 47.5 all-gather.16
  341.8 75.5 all-gather.24
  426.3 47.5 all-gather.18
  476.3 75.5 all-gather.26
